TPU v7x, 32 devices: a whole 2x2x4 slice. The times are simulated.
32 devices in a mesh: ctx: 4 (over z), head: 4 (over x, core), rep: 2 (over y).
Axes of the slice: x: 2, y: 2, z: 4, core: 2. Of those that a mesh axis runs over, the one named last changes fastest.
Arguments:
- queries: bfloat16 [4, 256, 2048], P('rep', 'ctx', 'head'), may hold values from -6 to 6
- keyvals: bfloat16 [4, 256, 4, 128], P('rep', 'ctx', 'head'), may hold values from -6 to 6
- sinks: float32 [32], P('head'), may hold values from -1 to 3
- stream: bfloat16 [4, 256, 2880], P('rep', 'ctx', 'head'), may hold values from -6 to 6
- out_weight: bfloat16 [2048, 2880], P('head', 'ctx'), may hold values from -0.75 to 0.75
- norm_gain: float32 [2880], replicated, may hold values from 0.1 to 1.9
- router: bfloat16 [2880, 32], replicated, may hold values from -0.12 to 0.12
- expert_ids: int32 [4, 256, 4], P('rep', 'ctx'), may hold values from 0 to 31, all different within a row; in each aligned block of 64 rows (0 to 63, 64 to 127, ..., all dimensions but the last counted through in order) at most 12 rows name the same one
- w_gate_up: bfloat16 [64, 720, 5760], P('ctx', 'head'), may hold values from -0.109375 to 0.109375
- w_down: bfloat16 [64, 720, 2880], P('ctx', None, 'head'), may hold values from -0.15625 to 0.15625
Outputs:
- layer_out: bfloat16 [4, 256, 2880], P('rep', 'ctx', 'head')
Inputs may be any that keep to these rules, and one draw needn't show every extreme that they name: `expert_ids`: each position names 4 different experts. Within each aligned block of 64 positions of a sequence no expert is named by more than 12 positions, and in every draw some block has an expert named by exactly 12.
All inputs are finite; a program needn't handle non-finite values.
Results may differ from a plain program's by a relative error of at most 0.015.
Values may be sent and summed in bfloat16 or wider, within the bound.
A program may use at most 192 MiB of HBM per device.

v0:
```python
import jax
import jax.numpy as jnp
from jax import lax
from jax.sharding import PartitionSpec as P


def on_device(
    queries, keyvals, sinks, stream, out_weight, norm_gain, router, expert_ids, w_gate_up, w_down
):
    ctx_count = lax.axis_size("ctx")
    rep_count = lax.axis_size("rep")
    local_seqs = queries.shape[0]
    tokens = queries.shape[1]
    row_count = local_seqs * tokens
    kv_local = keyvals.shape[2]
    head_dim = keyvals.shape[3] // 2
    q_local = queries.shape[2] // head_dim
    query_group_size = q_local // kv_local
    wide_rows = query_group_size * tokens
    col_width = stream.shape[2]
    first_pos = lax.axis_index("ctx") * tokens
    last_pos = first_pos + tokens - 1
    score_scale = head_dim ** (-0.5)
    scaled_queries = queries * jnp.asarray(score_scale, jnp.bfloat16)
    query_grid = scaled_queries.reshape(local_seqs, tokens, kv_local, query_group_size, head_dim)
    query_wide = jnp.transpose(query_grid, (0, 2, 3, 1, 4)).reshape(
        local_seqs, kv_local, wide_rows, head_dim
    )
    positions = first_pos + jnp.tile(jnp.arange(tokens), query_group_size)
    sink_rows = jnp.repeat(sinks.reshape(kv_local, query_group_size), tokens, axis=1)
    sink_grid = jnp.broadcast_to(sink_rows[None], (local_seqs, kv_local, wide_rows))
    start_state = (
        sink_grid,
        jnp.ones_like(sink_grid),
        jnp.zeros((local_seqs, kv_local, head_dim, wide_rows), jnp.float32),
    )
    gate_up_weights = w_gate_up.reshape(
        w_gate_up.shape[0], w_gate_up.shape[1], 2, w_gate_up.shape[2] // 2
    )

    def attend_block(running, shard_piece):
        peak_old, denom_old, accum_old = running
        key_block = shard_piece[..., :head_dim]
        value_block = shard_piece[..., head_dim:]
        scores = jnp.einsum(
            "skmd,snkd->sknm", query_wide, key_block, preferred_element_type=jnp.float32
        )
        key_pos = jnp.arange(shard_piece.shape[1])
        visible = key_pos[:, None] <= positions[None, :]
        masked = jnp.where(visible[None, None], scores, -jnp.inf)
        peak_new = jnp.maximum(peak_old, jnp.max(masked, axis=2))
        exp_terms = jnp.exp(masked - peak_new[:, :, None, :])
        factor = jnp.exp(peak_old - peak_new)
        denom_new = denom_old * factor + jnp.sum(exp_terms, axis=2)
        accum_new = accum_old * factor[:, :, None, :] + jnp.einsum(
            "sknm,snkd->skdm",
            exp_terms.astype(jnp.bfloat16),
            value_block,
            preferred_element_type=jnp.float32,
        )
        return (peak_new, denom_new, accum_new)

    shard_piece = lax.all_gather(keyvals, "ctx", axis=1, tiled=True)

    def keep_state(state_in):
        return state_in

    def update_state(state_in):
        return attend_block(state_in, shard_piece)

    peak_fin, denom_fin, accum_fin = lax.cond(
        jnp.int32(0) > last_pos, keep_state, update_state, start_state
    )
    normalized = (accum_fin / denom_fin[:, :, None, :]).reshape(
        local_seqs, kv_local, head_dim, query_group_size, tokens
    )
    attended = (
        jnp.transpose(normalized, (0, 4, 1, 3, 2))
        .reshape(row_count, q_local * head_dim)
        .astype(jnp.bfloat16)
    )
    partial_proj = jnp.dot(
        attended,
        lax.all_gather(out_weight, "ctx", axis=1, tiled=True),
        preferred_element_type=jnp.float32,
    )
    col_start = lax.axis_index("head") * col_width
    own_stream = stream.reshape(row_count, col_width).astype(jnp.float32)
    own_cols = lax.dynamic_slice_in_dim(partial_proj, col_start, col_width, 1) + own_stream
    placed = lax.dynamic_update_slice_in_dim(partial_proj, own_cols, col_start, 1)
    hidden_state = lax.psum(placed.astype(jnp.bfloat16), "head")
    state_float = hidden_state.astype(jnp.float32)
    inverse = lax.rsqrt(jnp.mean(state_float * state_float, axis=-1, keepdims=True) + 1e-05)
    send_rows = (state_float * inverse * norm_gain).astype(jnp.bfloat16)
    logits = jnp.dot(send_rows, router, preferred_element_type=jnp.float32)
    own_state = lax.dynamic_slice_in_dim(hidden_state, col_start, col_width, 1)
    expert_rows = expert_ids.reshape(row_count, expert_ids.shape[2])
    expert_count = router.shape[1]
    top_count = expert_rows.shape[1]
    member = expert_rows[:, :, None] == jnp.arange(expert_count)[None, None, :]
    chosen = jnp.sum(jnp.where(member, logits[:, None, :], 0.0), axis=-1)
    mix_weights = jax.nn.softmax(chosen, axis=-1)
    block_rows = row_count // rep_count
    member_int = member.astype(jnp.int32).reshape(rep_count, block_rows * top_count, expert_count)
    earlier = jnp.cumsum(member_int, axis=1) - member_int
    slot_rank = jnp.sum(earlier * member_int, axis=-1).reshape(row_count, top_count)
    target_rep = (jnp.arange(row_count) // block_rows)[:, None]
    local_halves = w_gate_up.shape[0]
    capacity = 3 * tokens // 16
    slot_total = ctx_count * rep_count * local_halves * capacity
    slot_lists = []
    for half_index in range(2):
        weight_row = 2 * expert_rows + half_index
        target_rank = weight_row // local_halves * rep_count + target_rep
        slot_lists.append(
            (target_rank * local_halves + weight_row % local_halves) * capacity + slot_rank
        )
    slot_index = jnp.stack(slot_lists, axis=-1)
    row_ids = jnp.broadcast_to(jnp.arange(row_count)[:, None, None], slot_index.shape)
    spread = (
        jnp.zeros((slot_total, row_count), jnp.bfloat16)
        .at[slot_index.reshape(-1), row_ids.reshape(-1)]
        .set(1.0)
    )
    outgoing = jnp.dot(spread, send_rows, preferred_element_type=jnp.float32).astype(jnp.bfloat16)
    outgoing = outgoing.reshape(ctx_count * rep_count, local_halves, capacity, send_rows.shape[1])
    gate_up = jnp.einsum(
        "sgcd,ghzd->sgczh",
        lax.all_to_all(outgoing, ("ctx", "rep"), split_axis=0, concat_axis=0, tiled=True),
        gate_up_weights,
        preferred_element_type=jnp.float32,
    )
    gate_part = gate_up[:, :, :, 0]
    up_part = gate_up[:, :, :, 1]
    active = (gate_part * jax.nn.sigmoid(1.702 * gate_part) * (up_part + 1.0)).astype(jnp.bfloat16)
    expert_out = jnp.einsum(
        "sgch,ghd->sgcd",
        lax.all_gather(active, "head", axis=3, tiled=True),
        w_down,
        preferred_element_type=jnp.float32,
    ).astype(jnp.bfloat16)
    returned = lax.all_to_all(expert_out, ("ctx", "rep"), split_axis=0, concat_axis=0, tiled=True)
    returned_rows = returned.reshape(slot_total, col_width)
    picked_rows = returned_rows[slot_index]
    combined = jnp.sum(mix_weights[:, :, None, None] * picked_rows.astype(jnp.float32), axis=(1, 2))
    layer_out = (own_state.astype(jnp.float32) + combined).astype(jnp.bfloat16)
    return layer_out.reshape(local_seqs, tokens, col_width)


def solution(mesh):
    placed = (
        P("rep", "ctx", "head"),
        P("rep", "ctx", "head", None),
        P("head"),
        P("rep", "ctx", "head"),
        P("head", "ctx"),
        P(),
        P(),
        P("rep", "ctx", None),
        P("ctx", "head", None),
        P("ctx", None, "head"),
    )
    return jax.shard_map(
        on_device, mesh=mesh, in_specs=placed, out_specs=P("rep", "ctx", "head"), check_vma=False
    )
```

profile of v0, /device:TPU:0, one launch (start us, length us, event | category | flops | bytes accessed | tf_op | source)
XLA Modules:
  0.0 662.0 jit_solution(3322971049654471776)
XLA Ops:
  6.5 0.7 all-gather.3.cloned.1.call-update
  7.3 0.8 copy.78
  8.3 0.7 broadcast_multiply_fusion.1
  9.1 0.8 copy.70
  9.9 1.2 reduce-window.6
  11.7 0.9 broadcast_multiply_fusion
  12.8 16.1 %all_gather.9 = bf16[2,256,1,128]{3,0,2,1:T(2,128)(2,1)S(1)} all-gather(bf16[2,64,1,128]{3,0,2,1:T(2,128)(2,1)S(1)} %copy.70), channel_id=1, replica_groups=mesh['ctx'=4,'head'=4,'rep'=2] {'ctx'}, dimensions={1}, use_global_device_ids=true | all-gather | bytes 163840 | tf_op jit(solution)/shard_map/all_gather | solution.py:63
  28.9 2.4 conditional.1
  28.9 0.3 copy.72
  29.4 0.7 broadcast_in_dim.35
  30.4 0.4 fusion.53
  31.0 0.3 fusion
  31.5 0.3 copy.73
  32.2 0.3 reshape.725
  32.5 0.3 reshape.726
  33.0 39.7 %all-gather.3.cloned.1.call-done = bf16[512,2880]{0,1:T(8,128)(2,1)} async-done(((bf16[512,720]{0,1:T(8,128)(2,1)}), bf16[512,2880]{0,1:T(8,128)(2,1)}) %all-gather.3.cloned.1.call-update) | async-done | bytes 2949136 | tf_op jit(solution)/shard_map/all_gather | solution.py:84
  72.8 2.8 fusion.54
  75.6 0.9 convert_element_type.70
  76.8 19.2 %scatter_custom_fusion = bf16[196608]{0:T(1024)(128)(2,1)S(1)} fusion(s32[1024]{0:T(1024)S(1)} %broadcast_select_fusion, bf16[1024]{0:T(1024)(128)(2,1)S(1)} %broadcast.896, bf16[]{:T(256)} %constant.105.clone.1), kind=kCustom, calls=%fused_computation.44 | custom fusion | bytes 393218
  96.1 13.8 %all-reduce.2.cloned.1.call-done = bf16[128,2880]{0,1:T(8,128)(2,1)} async-done(((bf16[128,2880]{0,1:T(8,128)(2,1)}), bf16[128,2880]{0,1:T(8,128)(2,1)}) %all-reduce.2.cloned.1.call-update) | async-done | bytes 737296 | tf_op jit(solution)/shard_map/psum | solution.py:91
  109.9 1.5 fusion.22
  111.5 7.0 %convolution_convert_fusion = bf16[1536,2880]{0,1:T(8,128)(2,1)} fusion(bf16[196608]{0:T(1024)(128)(2,1)S(1)} %scatter_custom_fusion, bf16[128,2880]{0,1:T(8,128)(2,1)} %all-reduce.2.cloned.1.call-done, f32[2880]{0:T(1024)S(1)} %copy-done.4, f32[128]{0:T(128)S(1)} %add_rsqrt_fusion), kind=kOutput, calls=%fused_computation.24 | convolution fusion | flops 1138360320 | bytes 9989888 | tf_op jit(solution)/shard_map/dot_general | solution.py:125
  118.5 12.5 %copy.84 = bf16[1536,2880]{1,0:T(8,128)(2,1)} copy(bf16[1536,2880]{0,1:T(8,128)(2,1)} %convolution_convert_fusion) | data formatting | bytes 17694720 | tf_op jit(solution)/shard_map/convert_element_type | solution.py:125
  131.0 13.4 %reshape.727 = bf16[8,16,12,2880]{3,2,1,0:T(8,128)(2,1)} reshape(bf16[1536,2880]{1,0:T(8,128)(2,1)} %copy.84) | data formatting | bytes 17694720 | tf_op jit(solution)/shard_map/reshape | solution.py:126
  144.4 9.7 %copy.85 = bf16[8,16,12,2880]{3,1,2,0:T(8,128)(2,1)} copy(bf16[8,16,12,2880]{3,2,1,0:T(8,128)(2,1)} %reshape.727) | data formatting | bytes 17694720 | tf_op jit(solution)/shard_map/reshape | solution.py:126
  154.1 5.5 all-to-all-start
  159.7 55.8 %reshape.728 = bf16[16,180,2,2880]{3,2,0,1:T(2,128)(2,1)} reshape(bf16[16,180,5760]{2,0,1:T(8,128)(2,1)} %param.20) | data formatting | bytes 66355200 | tf_op jit(solution)/shard_map/reshape | solution.py:37
  215.5 140.7 %all-to-all-done = bf16[8,16,12,2880]{3,1,2,0:T(8,128)(2,1)} async-done(((bf16[8,16,12,2880]{3,1,2,0:T(8,128)(2,1)}), bf16[8,16,12,2880]{3,1,2,0:T(8,128)(2,1)}, u32[]{:S(2)}, u32[]{:S(2)}) %all-to-all-start) | async-done | bytes 8847392 | tf_op jit(solution)/shard_map/all_to_all | solution.py:129
  356.2 43.2 %fusion.14 = f32[8,16,12,2,180]{4,2,3,0,1:T(8,128)S(1)} fusion(bf16[16,180,2,2880,1]{3,2,0,1,4:T(2,128)(2,1)} %bitcast.104, bf16[8,16,12,2880,1]{3,1,2,0,4:T(8,128)(2,1)} %bitcast.12), kind=kOutput, calls=%fused_computation.27 | convolution fusion | flops 3185049600 | bytes 44236800 | tf_op jit(solution)/shard_map/sgcd,ghzd->sgczh/dot_general | solution.py:127
  399.3 1.6 fusion.21
  401.0 14.9 %copy.89 = bf16[8,16,12,180]{1,0,2,3:T(8,128)(2,1)} copy(bf16[8,16,12,180]{3,2,0,1:T(8,128)(2,1)} %fusion.21) | data formatting | bytes 1105920 | tf_op jit(solution)/shard_map/convert_element_type | solution.py:135
  415.8 112.2 %all-gather.5.cloned.1.call-done = bf16[8,16,12,720]{1,0,2,3:T(8,128)(2,1)} async-done(((bf16[8,16,12,180]{1,0,2,3:T(8,128)(2,1)}), bf16[8,16,12,720]{1,0,2,3:T(8,128)(2,1)}) %all-gather.5.cloned.1.call-update) | async-done | bytes 2211856 | tf_op jit(solution)/shard_map/all_gather | solution.py:138
  528.1 34.0 %copy.90 = bf16[8,16,12,720]{3,2,0,1:T(8,128)(2,1)S(1)} copy(bf16[8,16,12,720]{1,0,2,3:T(8,128)(2,1)} %all-gather.5.cloned.1.call-done) | data formatting | bytes 4423680 | tf_op jit(solution)/shard_map/all_gather | solution.py:138
  562.1 8.8 %convert_bitcast_fusion = bf16[8,16,12,720]{3,2,0,1:T(8,128)(2,1)S(1)} fusion(bf16[8,16,12,720]{3,2,0,1:T(8,128)(2,1)S(1)} %copy.90, bf16[16,720,720]{2,1,0:T(8,128)(2,1)} %param.21), kind=kOutput, calls=%fused_computation.26 | convolution fusion | flops 1593630720 | bytes 21012480 | tf_op jit(solution)/shard_map/sgch,ghd->sgcd/dot_general | solution.py:136
  570.9 2.7 copy.91
  573.6 5.9 all-to-all-start.1
  579.6 0.7 eq.37
  580.7 1.3 fusion.27
  582.0 0.7 select_reduce_fusion
  582.9 50.9 %all-to-all-done.1 = bf16[8,16,12,720]{3,1,2,0:T(8,128)(2,1)S(1)} async-done(((bf16[8,16,12,720]{3,1,2,0:T(8,128)(2,1)}), bf16[8,16,12,720]{3,1,2,0:T(8,128)(2,1)S(1)}, u32[]{:S(2)}, u32[]{:S(2)}) %all-to-all-start.1) | async-done | bytes 2211872 | tf_op jit(solution)/shard_map/all_to_all | solution.py:142
  633.8 2.6 copy.92
  636.3 4.0 reshape.729
  640.3 5.2 gather_fusion
  645.6 3.5 reshape.751
  649.1 3.0 multiply_reduce_fusion
  652.0 1.2 copy.94
  653.2 1.0 add_convert_fusion
  654.2 0.8 copy.95
  (69 shorter events, 3.7 us)
Async XLA Ops:
  6.5 574.1 %copy-start = (bf16[2880,32]{0,1:T(8,128)(2,1)S(1)}, bf16[2880,32]{0,1:T(8,128)(2,1)}, u32[]{:S(2)}) copy-start(bf16[2880,32]{0,1:T(8,128)(2,1)} %param.18) | copy-start | bytes 552964
  6.5 66.2 %all-gather.3.cloned.1.call-start = ((), (), s32[]{:S(2)}) async-start(), calls=%async_computation.2 | async-start | bytes 3686400 | tf_op jit(solution)/shard_map/all_gather | solution.py:84
  7.3 102.7 %all-reduce.2.cloned.1.call-start = ((), (), s32[]{:S(2)}) async-start(), calls=%async_computation.3 | async-start | bytes 1474560 | tf_op jit(solution)/shard_map/psum | solution.py:91
  28.9 3.9 copy-start.2
  75.5 1.1 copy-start.7
  75.6 1.2 copy-start.6
  75.6 35.9 %copy-start.4 = (f32[2880]{0:T(1024)S(1)}, f32[2880]{0:T(1024)}, u32[]{:S(2)}) copy-start(f32[2880]{0:T(1024)} %param.17) | copy-start | bytes 34564
  111.4 7.1 %copy-start.5 = (f32[128]{0:T(128)}, f32[128]{0:T(128)S(1)}, u32[]{:S(2)}) copy-start(f32[128]{0:T(128)S(1)} %add_rsqrt_fusion) | copy-start | bytes 1540
  154.1 202.0 %all-to-all-start = ((bf16[8,16,12,2880]{3,1,2,0:T(8,128)(2,1)}), bf16[8,16,12,2880]{3,1,2,0:T(8,128)(2,1)}, u32[]{:S(2)}, u32[]{:S(2)}) async-start(bf16[8,16,12,2880]{3,1,2,0:T(8,128)(2,1)} %copy.85), calls=%async_computation | async-start | bytes 18087936 | tf_op jit(solution)/shard_map/all_to_all | solution.py:129
  159.7 368.4 %all-gather.5.cloned.1.call-start = ((), (), s32[]{:S(2)}) async-start(), calls=%async_computation.4 | async-start | bytes 22118400 | tf_op jit(solution)/shard_map/all_gather | solution.py:138
  573.6 5.9 copy-start.3
  573.6 7.1 %copy-start.1 = (bf16[128,2880]{0,1:T(8,128)(2,1)S(1)}, bf16[128,2880]{0,1:T(8,128)(2,1)}, u32[]{:S(2)}) copy-start(bf16[128,2880]{0,1:T(8,128)(2,1)} %all-reduce.2.cloned.1.call-done) | copy-start | bytes 2211844
  573.6 60.2 %all-to-all-start.1 = ((bf16[8,16,12,720]{3,1,2,0:T(8,128)(2,1)}), bf16[8,16,12,720]{3,1,2,0:T(8,128)(2,1)S(1)}, u32[]{:S(2)}, u32[]{:S(2)}) async-start(bf16[8,16,12,720]{3,1,2,0:T(8,128)(2,1)} %copy.91), calls=%async_computation.1 | async-start | bytes 4718592 | tf_op jit(solution)/shard_map/all_to_all | solution.py:142
Sparse Core Ops, SparseCore 0:
  8.9 63.8 all-gather.2
  76.7 33.1 all-reduce.1
  416.0 112.0 all-gather.4
where the time goes:
time: 671 us; the launch traced here: 662 us
  waiting for transfers between devices  358 us (53%)
  local copies, waits for them, and re-layouts  186 us (28%)
  matrix products  63.7 us (9%)
  blocking collectives  16.1 us (2%)
  between operations  13.9 us (2%)
  other arithmetic  12.4 us (2%)
  starting transfers between devices  11.5 us (2%)
    all_to_all x1, waiting for transfers between devices, on_device(): lax.all_to_all(outgoing, ('ctx', 'rep'), split_axis=0, concat_axis=0, til...  141 us
    all_gather x1, waiting for transfers between devices, on_device(): lax.all_gather(active, 'head', axis=3, tiled=True)  112 us
    reshape x1, local copies, waits for them, and re-layouts, on_device(): w_gate_up.reshape(w_gate_up.shape[0], w_gate_up.shape[1], 2, w_gate_up.sh...  55.8 us
    all_to_all x1, waiting for transfers between devices, on_device(): lax.all_to_all(expert_out, ('ctx', 'rep'), split_axis=0, concat_axis=0, t...  50.9 us
    dot_general x1, matrix products, on_device(): jnp.einsum('sgcd,ghzd->sgczh', lax.all_to_all(outgoing, ('ctx', 'rep'), s...  43.2 us
    all_gather x1, waiting for transfers between devices, on_device(): lax.all_gather(out_weight, 'ctx', axis=1, tiled=True)  39.7 us
    all_gather x1, local copies, waits for them, and re-layouts, on_device(): lax.all_gather(active, 'head', axis=3, tiled=True)  34 us
    reshape x2, local copies, waits for them, and re-layouts, on_device(): outgoing.reshape(ctx_count * rep_count, local_halves, capacity, send_rows...  23.2 us
  transfers between devices with their start and end apart: 5, of which 5 were waited for; matrix products, arithmetic and copies ran while one was open for 13% of the time, Pallas kernels for 0%

commit v1 on v0

v1 whole, which is shorter than its diff:
```python
import functools

import jax
import jax.numpy as jnp
from jax import lax
from jax.experimental import pallas as pl
from jax.experimental.pallas import tpu as pltpu
from jax.sharding import PartitionSpec as P


NT = (((1,), (1,)), ((), ()))
TN = (((0,), (0,)), ((), ()))
LANES = 128


def one_hot_rows(slots, cap, value):
    rows = lax.broadcasted_iota(jnp.int32, (cap, slots.shape[1]), 0)
    return jnp.where(rows == slots, value, 0.0).astype(jnp.bfloat16)


def gate_up_kernel(
    halves,
    units,
    state_ref,
    gain_ref,
    router_ref,
    w_ref,
    slot_ref,
    out_ref,
    logits_ref,
    act_ref,
    xg_ref,
    xu_ref,
):
    step = pl.program_id(1)
    groups, shards, group_rows, cols = state_ref.shape

    @pl.when(step == 0)
    def _():
        for group in range(groups):
            pieces = [state_ref[group, shard].astype(jnp.float32) for shard in range(shards)]
            square = sum(jnp.sum(piece * piece, axis=1, keepdims=True) for piece in pieces)
            inverse = lax.rsqrt(square / (shards * cols) + 1e-05)
            scaled = [
                (piece * inverse * gain_ref[shard]).astype(jnp.bfloat16)
                for shard, piece in enumerate(pieces)
            ]
            extra = xg_ref.shape[1] - shards * cols
            blank = [jnp.zeros((group_rows, extra), jnp.bfloat16)] if extra else []
            here = slice(group * group_rows, (group + 1) * group_rows)
            xg_ref[here, :] = jnp.concatenate(scaled + blank, axis=1)
            xu_ref[here, :] = jnp.concatenate(blank + scaled, axis=1)
        logits_ref[...] = lax.dot_general(
            router_ref[...], xg_ref[...], NT, preferred_element_type=jnp.float32
        )

    rows, wide = w_ref.shape[0], xg_ref.shape[1]
    gate = lax.dot_general(w_ref[:, :wide], xg_ref[...], NT, preferred_element_type=jnp.float32)
    up = lax.dot_general(
        w_ref[:, w_ref.shape[1] - wide :], xu_ref[...], NT, preferred_element_type=jnp.float32
    )
    active = gate * jax.nn.sigmoid(1.702 * gate) * (up + 1.0)
    slabs = act_ref.shape[0]
    for slab in range(slabs):
        act_ref[slab, pl.ds(step * rows, rows), :] = active[:, slab * LANES : (slab + 1) * LANES]

    @pl.when(step == pl.num_programs(1) - 1)
    def _():
        for row in range(halves):
            wanted = pl.ds(row, units, stride=halves) if halves > 1 else pl.ds(0, units)
            picked = jnp.concatenate([act_ref[slab, wanted, :] for slab in range(slabs)], axis=1)
            spread = one_hot_rows(slot_ref[row], out_ref.shape[2], 1.0)
            out_ref[row, 0] = lax.dot_general(
                spread, picked.astype(jnp.bfloat16), NT, preferred_element_type=jnp.float32
            ).astype(jnp.bfloat16)


def gate_up_call(state, gain, router, weights, slots, units, token_block, cap):
    halves = slots.shape[0]
    sources, shards, group_rows, cols = state.shape
    groups = token_block // group_rows
    blocks = sources // groups
    experts, wide = router.shape
    wide_w = weights.shape[1]
    sizes = [
        size
        for size in range(1, units + 1)
        if units % size == 0
        and (size == units or (size * halves) % 16 == 0)
        and size * halves * wide_w * 2 <= 4 << 20
    ]
    size = sizes[-1]
    return pl.pallas_call(
        functools.partial(gate_up_kernel, halves, units),
        grid=(blocks, units // size),
        out_shape=(
            jax.ShapeDtypeStruct((halves, blocks, cap, units), jnp.bfloat16),
            jax.ShapeDtypeStruct((experts, blocks * token_block), jnp.float32),
        ),
        in_specs=[
            pl.BlockSpec((groups, shards, group_rows, cols), lambda i, j: (i, 0, 0, 0)),
            pl.BlockSpec((shards, 1, cols), lambda i, j: (0, 0, 0)),
            pl.BlockSpec((experts, wide), lambda i, j: (0, 0)),
            pl.BlockSpec((size * halves, wide_w), lambda i, j: (j, 0)),
            pl.BlockSpec((halves, 1, token_block), lambda i, j: (0, 0, i)),
        ],
        out_specs=(
            pl.BlockSpec((halves, 1, cap, units), lambda i, j: (0, i, 0, 0)),
            pl.BlockSpec((experts, token_block), lambda i, j: (0, i)),
        ),
        scratch_shapes=[
            pltpu.VMEM((token_block // LANES, units * halves, LANES), jnp.float32),
            pltpu.VMEM((token_block, wide), jnp.bfloat16),
            pltpu.VMEM((token_block, wide), jnp.bfloat16),
        ],
        compiler_params=pltpu.CompilerParams(vmem_limit_bytes=56 << 20),
    )(state, gain, router, weights, slots)


def down_kernel(act_ref, place_ref, w_ref, slot_ref, mix_ref, out_ref, total_ref):
    row = pl.program_id(1)
    hidden = None
    for shard in range(act_ref.shape[0]):
        piece = jnp.dot(
            act_ref[shard, 0, 0], place_ref[shard], preferred_element_type=jnp.float32
        )
        hidden = piece if hidden is None else hidden + piece
    part = jnp.dot(hidden.astype(jnp.bfloat16), w_ref[0], preferred_element_type=jnp.float32)
    spread = one_hot_rows(slot_ref[0], act_ref.shape[3], mix_ref[0])
    added = lax.dot_general(
        spread, part.astype(jnp.bfloat16), TN, preferred_element_type=jnp.float32
    )

    @pl.when(row == 0)
    def _():
        total_ref[...] = added

    @pl.when(row != 0)
    def _():
        total_ref[...] += added

    @pl.when(row == pl.num_programs(1) - 1)
    def _():
        out_ref[...] = total_ref[...].astype(jnp.bfloat16)


def down_call(act, weights, slots, mix, token_block):
    shards, halves, blocks, cap, units = act.shape
    hidden, cols = weights.shape[1:]
    at = lax.broadcasted_iota(jnp.int32, (shards, units, hidden), 0) * units
    at = at + lax.broadcasted_iota(jnp.int32, (shards, units, hidden), 1)
    place = (at == lax.broadcasted_iota(jnp.int32, (shards, units, hidden), 2)).astype(jnp.bfloat16)
    return pl.pallas_call(
        down_kernel,
        grid=(blocks, halves),
        out_shape=jax.ShapeDtypeStruct((blocks * token_block, cols), jnp.bfloat16),
        in_specs=[
            pl.BlockSpec((shards, 1, 1, cap, units), lambda i, r: (0, r, i, 0, 0)),
            pl.BlockSpec((shards, units, hidden), lambda i, r: (0, 0, 0)),
            pl.BlockSpec((1, hidden, cols), lambda i, r: (r, 0, 0)),
            pl.BlockSpec((1, 1, token_block), lambda i, r: (r, 0, i)),
            pl.BlockSpec((1, 1, token_block), lambda i, r: (r, 0, i)),
        ],
        out_specs=pl.BlockSpec((token_block, cols), lambda i, r: (i, 0)),
        scratch_shapes=[pltpu.VMEM((token_block, cols), jnp.float32)],
        compiler_params=pltpu.CompilerParams(vmem_limit_bytes=48 << 20),
    )(act, place, weights, slots, mix)


def on_device(
    queries, keyvals, sinks, stream, out_weight, norm_gain, router, expert_ids, w_gate_up, w_down
):
    ctx_count = lax.axis_size("ctx")
    local_seqs = queries.shape[0]
    tokens = queries.shape[1]
    row_count = local_seqs * tokens
    kv_local = keyvals.shape[2]
    head_dim = keyvals.shape[3] // 2
    q_local = queries.shape[2] // head_dim
    query_group_size = q_local // kv_local
    wide_rows = query_group_size * tokens
    col_width = stream.shape[2]
    first_pos = lax.axis_index("ctx") * tokens
    last_pos = first_pos + tokens - 1
    score_scale = head_dim ** (-0.5)
    scaled_queries = queries * jnp.asarray(score_scale, jnp.bfloat16)
    query_grid = scaled_queries.reshape(local_seqs, tokens, kv_local, query_group_size, head_dim)
    query_wide = jnp.transpose(query_grid, (0, 2, 3, 1, 4)).reshape(
        local_seqs, kv_local, wide_rows, head_dim
    )
    positions = first_pos + jnp.tile(jnp.arange(tokens), query_group_size)
    sink_rows = jnp.repeat(sinks.reshape(kv_local, query_group_size), tokens, axis=1)
    sink_grid = jnp.broadcast_to(sink_rows[None], (local_seqs, kv_local, wide_rows))
    start_state = (
        sink_grid,
        jnp.ones_like(sink_grid),
        jnp.zeros((local_seqs, kv_local, head_dim, wide_rows), jnp.float32),
    )

    def attend_block(running, shard_piece):
        peak_old, denom_old, accum_old = running
        key_block = shard_piece[..., :head_dim]
        value_block = shard_piece[..., head_dim:]
        scores = jnp.einsum(
            "skmd,snkd->sknm", query_wide, key_block, preferred_element_type=jnp.float32
        )
        key_pos = jnp.arange(shard_piece.shape[1])
        visible = key_pos[:, None] <= positions[None, :]
        masked = jnp.where(visible[None, None], scores, -jnp.inf)
        peak_new = jnp.maximum(peak_old, jnp.max(masked, axis=2))
        exp_terms = jnp.exp(masked - peak_new[:, :, None, :])
        factor = jnp.exp(peak_old - peak_new)
        denom_new = denom_old * factor + jnp.sum(exp_terms, axis=2)
        accum_new = accum_old * factor[:, :, None, :] + jnp.einsum(
            "sknm,snkd->skdm",
            exp_terms.astype(jnp.bfloat16),
            value_block,
            preferred_element_type=jnp.float32,
        )
        return (peak_new, denom_new, accum_new)

    shard_piece = lax.all_gather(keyvals, "ctx", axis=1, tiled=True)

    def keep_state(state_in):
        return state_in

    def update_state(state_in):
        return attend_block(state_in, shard_piece)

    peak_fin, denom_fin, accum_fin = lax.cond(
        jnp.int32(0) > last_pos, keep_state, update_state, start_state
    )
    normalized = (accum_fin / denom_fin[:, :, None, :]).reshape(
        local_seqs, kv_local, head_dim, query_group_size, tokens
    )
    attended = (
        jnp.transpose(normalized, (0, 4, 1, 3, 2))
        .reshape(row_count, q_local * head_dim)
        .astype(jnp.bfloat16)
    )
    partial_proj = jnp.dot(
        attended,
        lax.all_gather(out_weight, "ctx", axis=1, tiled=True),
        preferred_element_type=jnp.float32,
    )
    own_stream = stream.reshape(row_count, col_width).astype(jnp.float32)
    summed = lax.psum_scatter(
        partial_proj.astype(jnp.bfloat16), "head", scatter_dimension=1, tiled=True
    )
    own_state = (summed.astype(jnp.float32) + own_stream).astype(jnp.bfloat16)
    width = norm_gain.shape[0]
    every_state = lax.all_gather(own_state, ("ctx", "head"), axis=0, tiled=False)
    every_state = every_state.reshape(ctx_count, width // col_width, row_count, col_width)
    all_rows = ctx_count * row_count
    expert_count = router.shape[1]
    token_ids = lax.all_gather(
        expert_ids.reshape(row_count, expert_ids.shape[2]).T, "ctx", axis=1, tiled=True
    )
    halves = w_gate_up.shape[0]
    units = w_gate_up.shape[1]
    token_block = min(all_rows, 8 * tokens)
    cap = token_block // tokens * (3 * tokens // 16)
    row_expert = (lax.axis_index("ctx") * halves + jnp.arange(halves)) // 2
    named = jnp.any(token_ids[:, None, :] == row_expert[None, :, None], axis=0)
    counted = named.astype(jnp.int32).reshape(halves, all_rows // token_block, token_block)
    rank = jnp.cumsum(counted, axis=2) - 1
    slots = jnp.where(named, rank.reshape(halves, all_rows), -1).reshape(halves, 1, all_rows)
    unit_rows = jnp.transpose(w_gate_up, (1, 0, 2)).reshape(units * halves, w_gate_up.shape[2])
    router_rows = jnp.pad(router.T, ((0, 0), (0, -width % LANES)))
    gain = norm_gain.reshape(width // col_width, 1, col_width)
    active, logits = gate_up_call(
        every_state, gain, router_rows, unit_rows, slots, units, token_block, cap
    )
    member = jnp.any(token_ids[:, None, :] == jnp.arange(expert_count)[None, :, None], axis=0)
    masked = jnp.where(member, logits, -jnp.inf)
    mix_all = jax.nn.softmax(masked, axis=0)
    chosen_rows = (row_expert[:, None] == jnp.arange(expert_count)[None, :]).astype(jnp.float32)
    mix_rows = jnp.dot(chosen_rows, mix_all, precision=lax.Precision.HIGHEST)
    mix_rows = mix_rows.reshape(halves, 1, all_rows)
    every_active = lax.all_gather(active, "head", axis=0, tiled=False)
    partial_out = down_call(every_active, w_down, slots, mix_rows, token_block)
    combined = lax.psum_scatter(partial_out, "ctx", scatter_dimension=0, tiled=True)
    layer_out = (own_state.astype(jnp.float32) + combined.astype(jnp.float32)).astype(jnp.bfloat16)
    return layer_out.reshape(local_seqs, tokens, col_width)


def solution(mesh):
    placed = (
        P("rep", "ctx", "head"),
        P("rep", "ctx", "head", None),
        P("head"),
        P("rep", "ctx", "head"),
        P("head", "ctx"),
        P(),
        P(),
        P("rep", "ctx", None),
        P("ctx", "head", None),
        P("ctx", None, "head"),
    )
    return jax.shard_map(
        on_device, mesh=mesh, in_specs=placed, out_specs=P("rep", "ctx", "head"), check_vma=False
    )
```

time: 671 us -> 262 us (0.39); the launches traced: 662 us -> 261 us
  waiting for transfers between devices: 358 us -> 145 us
  local copies, waits for them, and re-layouts: 186 us -> 15.1 us
  matrix products: 63.7 us -> 4.49 us
  Pallas kernels: 0 us -> 48.4 us
  starting transfers between devices: 11.5 us -> 0.35 us
  blocking collectives: 16.1 us -> 27.2 us
    all_to_all x2 -> x0, waiting for transfers between devices: 192 us -> none  [the longest x1 141 us: on_device(): lax.all_to_all(outgoing, ('ctx', 'rep'), split_axis=0, concat_axis=0, til...]
    reshape x8 -> x3, local copies, waits for them, and re-layouts: 83.6 us -> 0.8 us  [the longest x1 0.69 us: on_device(): gain = norm_gain.reshape(width // col_width, 1, col_width)]
    dot_general x4 -> x1, matrix products: 60.3 us -> 0.2 us  [on_device(): mix_rows = jnp.dot(chosen_rows, mix_all, precision=lax.Precision.HIGHEST)]
    all_gather x1 -> x2, waiting for transfers between devices: 112 us -> 54.3 us  [the longest x1 30.1 us: on_device(): lax.all_gather(own_state, ('ctx', 'head'), axis=0, tiled=False)]
    pallas_call x0 -> x2, Pallas kernels: none -> 48.4 us  [the longest x1 28.5 us: gate_up_call(): pl.pallas_call(functools.partial(gate_up_kernel, halves, units), grid=(bl...]
    convert_element_type x6 -> x2, local copies, waits for them, and re-layouts: 34.5 us -> 0.02 us  [on_device(): named.astype(jnp.int32)]
    all_gather x1, local copies, waits for them, and re-layouts: 34 us -> 4.22 us  [on_device(): every_active = lax.all_gather(active, 'head', axis=0, tiled=False)]
    reduce_scatter x0 -> x1, waiting for transfers between devices: none -> 23.3 us  [on_device(): lax.psum_scatter(partial_out, 'ctx', scatter_dimension=0, tiled=True)]
  transfers between devices with their start and end apart: 5 -> 5, of which waited for: 5 -> 5; matrix products, arithmetic and copies ran while one was open for 13% -> 4% of each run, Pallas kernels for 0% -> 0%
where the time goes in v1:
time: 262 us; the launch traced here: 261 us
  waiting for transfers between devices  145 us (55%)
  Pallas kernels  48.4 us (18%)
  blocking collectives  27.2 us (10%)
  local copies, waits for them, and re-layouts  15.1 us (6%)
  between operations  13.4 us (5%)
  other arithmetic  7.18 us (3%)
  matrix products  4.49 us (2%)
    all_gather x1, waiting for transfers between devices, on_device(): lax.all_gather(out_weight, 'ctx', axis=1, tiled=True)  44.5 us
    all_gather x1, waiting for transfers between devices, on_device(): lax.all_gather(own_state, ('ctx', 'head'), axis=0, tiled=False)  30.1 us
    pallas_call x1, Pallas kernels, gate_up_call(): pl.pallas_call(functools.partial(gate_up_kernel, halves, units), grid=(bl...  28.5 us
    all_gather x1, waiting for transfers between devices, on_device(): every_active = lax.all_gather(active, 'head', axis=0, tiled=False)  24.2 us
    reduce_scatter x1, waiting for transfers between devices, on_device(): lax.psum_scatter(partial_out, 'ctx', scatter_dimension=0, tiled=True)  23.3 us
    unnamed x6, waiting for transfers between devices  22.5 us
    pallas_call x1, Pallas kernels, down_call(): pl.pallas_call(down_kernel, grid=(blocks, halves), out_shape=jax.ShapeDty...  19.9 us
    all_gather x1, blocking collectives, on_device(): shard_piece = lax.all_gather(keyvals, 'ctx', axis=1, tiled=True)  15.3 us
  transfers between devices with their start and end apart: 5, of which 5 were waited for; matrix products, arithmetic and copies ran while one was open for 4% of the time, Pallas kernels for 0%

profile of v1, /device:TPU:0, one launch (start us, length us, event | category | flops | bytes accessed | tf_op | source)
XLA Modules:
  0.0 260.7 jit_solution(3206678281753556861)
XLA Ops:
  6.5 0.7 all-gather.6.cloned.1.call-update
  7.3 0.9 broadcast_multiply_fusion
  8.2 0.2 reshape.281
  8.4 0.8 copy.40
  9.2 15.3 %all_gather.21 = bf16[2,256,1,128]{3,0,2,1:T(2,128)(2,1)S(1)} all-gather(bf16[2,64,1,128]{3,0,2,1:T(2,128)(2,1)S(1)} %copy.40), channel_id=1, replica_groups=mesh['ctx'=4,'head'=4,'rep'=2] {'ctx'}, dimensions={1}, use_global_device_ids=true | all-gather | bytes 163840 | tf_op jit(solution)/shard_map/all_gather | solution.py:222
  24.5 2.4 conditional.1
  24.5 0.1 copy.41
  24.6 0.2 copy.42
  24.9 0.2 reshape.268
  25.1 0.1 add.70
  25.2 0.1 iota_compare_fusion
  25.3 0.4 fusion.19
  25.6 0.7 broadcast_in_dim.29
  26.4 0.1 broadcast_in_dim.30
  26.5 0.3 fusion
  26.8 0.2 fusion.2
  27.0 0.2 convert_element_type.64
  27.2 0.2 copy.43
  27.4 0.2 convert_element_type.66
  27.7 44.5 %all-gather.6.cloned.1.call-done = bf16[512,2880]{0,1:T(8,128)(2,1)} async-done(((bf16[512,720]{0,1:T(8,128)(2,1)}), bf16[512,2880]{0,1:T(8,128)(2,1)}) %all-gather.6.cloned.1.call-update) | async-done | bytes 2949136 | tf_op jit(solution)/shard_map/all_gather | solution.py:243
  72.2 3.6 %fusion.7 = bf16[2880,128]{1,0:T(8,128)(2,1)} fusion(bf16[128,512]{1,0:T(8,128)(2,1)S(1)} %convert_element_type.66, bf16[512,2880]{0,1:T(8,128)(2,1)} %all-gather.6.cloned.1.call-done), kind=kOutput, calls=%fused_computation.18 | convolution fusion | flops 377856000 | bytes 3817472 | tf_op jit(solution)/shard_map/dot_general | solution.py:241
  75.8 0.0 all-gather.8.cloned.1.call-start
  75.9 21.8 %reduce-scatter.7.cloned.1.call-done = bf16[720,128]{1,0:T(8,128)(2,1)} async-done(((bf16[2880,128]{1,0:T(8,128)(2,1)}), bf16[720,128]{1,0:T(8,128)(2,1)}) %reduce-scatter.7.cloned.1.call-update) | async-done | bytes 184336
  97.6 1.1 copy.53
  98.7 0.7 fusion.9
  99.5 0.1 reshape.285
  99.6 12.0 %all_gather.25 = s32[4,512]{1,0:T(4,128)S(1)} all-gather(s32[4,128]{1,0:T(4,128)S(1)} %bitcast.73), channel_id=1, replica_groups=mesh['ctx'=4,'head'=4,'rep'=2] {'ctx'}, dimensions={1}, use_global_device_ids=true | all-gather | bytes 10240 | tf_op jit(solution)/shard_map/all_gather | solution.py:256
  111.6 0.1 compare_reduce_fusion
  111.7 1.2 reduce-window.6
  112.9 0.2 slice_reduce_fusion
  113.1 0.1 copy.48
  113.2 0.7 reshape.283.gain_ref
  113.9 0.7 pad.4.router_ref
  114.6 0.1 broadcast.172
  114.7 0.7 copy_select_fusion.slot_ref
  115.4 30.1 %all-gather.8.cloned.1.call-done = bf16[2048,720]{1,0:T(8,128)(2,1)} async-done(((bf16[128,720]{1,0:T(8,128)(2,1)}), bf16[2048,720]{1,0:T(8,128)(2,1)}) %all-gather.8.cloned.1.call-update) | async-done | bytes 2949136 | tf_op jit(solution)/shard_map/all_gather | solution.py:252
  145.5 28.5 %shard_map.101 = (bf16[16,1,96,180]{3,2,1,0:T(8,128)(2,1)}, f32[32,512]{1,0:T(8,128)}) custom-call(bf16[4,4,128,720]{3,2,1,0:T(8,128)(2,1)} %bitcast.64, f32[4,1,720]{2,1,0:T(1,128)} %reshape.283.gain_ref, bf16[32,2944]{1,0:T(8,128)(2,1)} %pad.4.router_ref, bf16[2880,5760]{1,0:T(8,128)(2,1)} %bitcast.63, s32[16,1,512]{2,1,0:T(1,128)} %copy_select_fusion.slot_ref), custom_call_target="tpu_custom_call" | custom-call | tf_op jit(solution)/shard_map/pallas_call | solution.py:93
  174.0 2.7 %copy.50 = bf16[16,1,96,180]{2,0,3,1:T(8,128)(2,1)} copy(bf16[16,1,96,180]{3,2,1,0:T(8,128)(2,1)} %get-tuple-element.33) | data formatting | bytes 1105920 | tf_op jit(solution)/shard_map/pallas_call | solution.py:93
  176.7 0.2 reduce-scatter.5.cloned.1.call-start
  177.0 1.5 fusion.8.place_ref
  178.5 0.2 fusion.11
  178.8 24.2 %all-gather.10.cloned.1.call-done = bf16[64,1,96,180]{2,0,3,1:T(8,128)(2,1)} async-done(((bf16[16,1,96,180]{2,0,3,1:T(8,128)(2,1)}), bf16[64,1,96,180]{2,0,3,1:T(8,128)(2,1)}) %all-gather.10.cloned.1.call-update) | async-done | bytes 2211856 | tf_op jit(solution)/shard_map/all_gather | solution.py:280
  203.0 4.2 %copy.51 = bf16[64,1,96,180]{3,2,0,1:T(8,128)(2,1)S(1)} copy(bf16[64,1,96,180]{2,0,3,1:T(8,128)(2,1)} %all-gather.10.cloned.1.call-done) | data formatting | bytes 4423680 | tf_op jit(solution)/shard_map/all_gather | solution.py:280
  207.2 1.2 copy-done
  208.5 19.9 %shard_map.102 = bf16[512,720]{1,0:T(8,128)(2,1)S(1)} custom-call(bf16[4,16,1,96,180]{4,3,2,1,0:T(8,128)(2,1)S(1)} %bitcast.62, bf16[4,180,720]{2,1,0:T(8,128)(2,1)S(1)} %copy-done, bf16[16,720,720]{2,1,0:T(8,128)(2,1)} %w_ref.1, s32[16,1,512]{2,1,0:T(1,128)S(1)} %copy-done.2, f32[16,1,512]{2,1,0:T(1,128)S(1)} %reshape.290.mix_ref), custom_call_target="tpu_custom_call" | custom-call | tf_op jit(solution)/shard_map/pallas_call | solution.py:153
  228.3 0.9 copy-done.1
  229.2 23.3 %reduce-scatter.5.cloned.1.call-done = bf16[128,720]{1,0:T(8,128)(2,1)} async-done(((bf16[512,720]{1,0:T(8,128)(2,1)}), bf16[128,720]{1,0:T(8,128)(2,1)}) %reduce-scatter.5.cloned.1.call-update) | async-done | bytes 184336 | tf_op jit(solution)/shard_map/reduce_scatter | solution.py:282
  252.5 1.6 add_convert_fusion
  (41 shorter events, 0.5 us)
Async XLA Ops:
  6.5 65.6 %all-gather.6.cloned.1.call-start = ((), (), s32[]{:S(2)}) async-start(), calls=%async_computation.2 | async-start | bytes 3686400 | tf_op jit(solution)/shard_map/all_gather | solution.py:243
  7.3 90.4 %reduce-scatter.7.cloned.1.call-start = ((), (), s32[]{:S(2)}) async-start(), calls=%async_computation.6 | async-start | bytes 921600
  27.2 71.5 %copy-start.5 = (bf16[2,64,720]{2,1,0:T(8,128)(2,1)S(1)}, bf16[2,64,720]{2,1,0:T(8,128)(2,1)}, u32[]{:S(2)}) copy-start(bf16[2,64,720]{2,1,0:T(8,128)(2,1)} %param.15) | copy-start | bytes 552964
  27.7 71.9 %copy-start.8 = (s32[2,64,4]{1,2,0:T(4,128)S(1)}, s32[2,64,4]{1,2,0:T(4,128)}, u32[]{:S(2)}) copy-start(s32[2,64,4]{1,2,0:T(4,128)} %param.19) | copy-start | bytes 6148
  27.7 85.6 %copy-start.7 = (f32[2880]{0:T(1024)S(1)}, f32[2880]{0:T(1024)}, u32[]{:S(2)}) copy-start(f32[2880]{0:T(1024)} %param.17) | copy-start | bytes 34564
  27.7 86.3 %copy-start.6 = (bf16[2880,32]{0,1:T(8,128)(2,1)S(1)}, bf16[2880,32]{0,1:T(8,128)(2,1)}, u32[]{:S(2)}) copy-start(bf16[2880,32]{0,1:T(8,128)(2,1)} %param.18) | copy-start | bytes 552964
  75.8 69.7 %all-gather.8.cloned.1.call-start = ((), (), s32[]{:S(2)}) async-start(), calls=%async_computation.4 | async-start | bytes 3342336 | tf_op jit(solution)/shard_map/all_gather | solution.py:252
  99.5 103.5 %all-gather.10.cloned.1.call-start = ((), (), s32[]{:S(2)}) async-start(), calls=%async_computation.5 | async-start | bytes 3686400 | tf_op jit(solution)/shard_map/all_gather | solution.py:280
  174.0 4.5 %copy-start.4 = (f32[32,512]{1,0:T(8,128)S(1)}, f32[32,512]{1,0:T(8,128)}, u32[]{:S(2)}) copy-start(f32[32,512]{1,0:T(8,128)} %get-tuple-element.34) | copy-start | bytes 196612
  176.7 75.9 %reduce-scatter.5.cloned.1.call-start = ((), (), s32[]{:S(2)}) async-start(), calls=%async_computation.3 | async-start | bytes 983040 | tf_op jit(solution)/shard_map/reduce_scatter | solution.py:282
  178.8 28.4 %copy-start.2 = (s32[16,1,512]{2,1,0:T(1,128)S(1)}, s32[16,1,512]{2,1,0:T(1,128)}, u32[]{:S(2)}) copy-start(s32[16,1,512]{2,1,0:T(1,128)} %copy_select_fusion.slot_ref) | copy-start | bytes 98308
  207.2 1.3 copy-start
  208.5 44.1 %copy-start.3 = (bf16[128,720]{1,0:T(8,128)(2,1)S(1)}, bf16[128,720]{1,0:T(8,128)(2,1)}, u32[]{:S(2)}) copy-start(bf16[128,720]{1,0:T(8,128)(2,1)} %fusion.9) | copy-start | bytes 552964
  228.3 0.9 copy-start.1
Sparse Core Ops, SparseCore 0:
  8.9 63.2 all-gather.5
  75.9 21.6 reduce-scatter.6
  99.9 45.4 all-gather.7
  176.8 26.1 all-gather.9
  229.4 23.1 reduce-scatter.4

commit v2 on v1

--- a/solution.py
+++ b/solution.py
@@ -117,29 +117,28 @@
     )(state, gain, router, weights, slots)
 
 
-def down_kernel(act_ref, place_ref, w_ref, slot_ref, mix_ref, out_ref, total_ref):
-    row = pl.program_id(1)
-    hidden = None
-    for shard in range(act_ref.shape[0]):
-        piece = jnp.dot(
-            act_ref[shard, 0, 0], place_ref[shard], preferred_element_type=jnp.float32
-        )
-        hidden = piece if hidden is None else hidden + piece
-    part = jnp.dot(hidden.astype(jnp.bfloat16), w_ref[0], preferred_element_type=jnp.float32)
+def down_kernel(act_ref, w_ref, slot_ref, mix_ref, out_ref, total_ref):
+    step = pl.program_id(1)
+    part = None
+    for row in range(w_ref.shape[0]):
+        pieces = [act_ref[shard, row, 0] for shard in range(act_ref.shape[0])]
+        hidden = jnp.concatenate(pieces, axis=1)
+        piece = jnp.dot(hidden, w_ref[row], preferred_element_type=jnp.float32)
+        part = piece if part is None else part + piece
     spread = one_hot_rows(slot_ref[0], act_ref.shape[3], mix_ref[0])
     added = lax.dot_general(
         spread, part.astype(jnp.bfloat16), TN, preferred_element_type=jnp.float32
     )
 
-    @pl.when(row == 0)
+    @pl.when(step == 0)
     def _():
         total_ref[...] = added
 
-    @pl.when(row != 0)
+    @pl.when(step != 0)
     def _():
         total_ref[...] += added
 
-    @pl.when(row == pl.num_programs(1) - 1)
+    @pl.when(step == pl.num_programs(1) - 1)
     def _():
         out_ref[...] = total_ref[...].astype(jnp.bfloat16)
 
@@ -147,30 +146,36 @@
 def down_call(act, weights, slots, mix, token_block):
     shards, halves, blocks, cap, units = act.shape
     hidden, cols = weights.shape[1:]
-    at = lax.broadcasted_iota(jnp.int32, (shards, units, hidden), 0) * units
-    at = at + lax.broadcasted_iota(jnp.int32, (shards, units, hidden), 1)
-    place = (at == lax.broadcasted_iota(jnp.int32, (shards, units, hidden), 2)).astype(jnp.bfloat16)
+    pair = 2 if halves % 2 == 0 else 1
     return pl.pallas_call(
         down_kernel,
-        grid=(blocks, halves),
+        grid=(blocks, halves // pair),
         out_shape=jax.ShapeDtypeStruct((blocks * token_block, cols), jnp.bfloat16),
         in_specs=[
-            pl.BlockSpec((shards, 1, 1, cap, units), lambda i, r: (0, r, i, 0, 0)),
-            pl.BlockSpec((shards, units, hidden), lambda i, r: (0, 0, 0)),
-            pl.BlockSpec((1, hidden, cols), lambda i, r: (r, 0, 0)),
-            pl.BlockSpec((1, 1, token_block), lambda i, r: (r, 0, i)),
-            pl.BlockSpec((1, 1, token_block), lambda i, r: (r, 0, i)),
+            pl.BlockSpec((shards, pair, 1, cap, units), lambda i, r: (0, r, i, 0, 0)),
+            pl.BlockSpec((pair, hidden, cols), lambda i, r: (r, 0, 0)),
+            pl.BlockSpec((1, 1, token_block), lambda i, r: (r * pair, 0, i)),
+            pl.BlockSpec((1, 1, token_block), lambda i, r: (r * pair, 0, i)),
         ],
         out_specs=pl.BlockSpec((token_block, cols), lambda i, r: (i, 0)),
         scratch_shapes=[pltpu.VMEM((token_block, cols), jnp.float32)],
         compiler_params=pltpu.CompilerParams(vmem_limit_bytes=48 << 20),
-    )(act, place, weights, slots, mix)
+    )(act, weights, slots, mix)
 
 
 def on_device(
     queries, keyvals, sinks, stream, out_weight, norm_gain, router, expert_ids, w_gate_up, w_down
 ):
     ctx_count = lax.axis_size("ctx")
+    rep_count = lax.axis_size("rep")
+    share = out_weight.shape[1] // rep_count
+    if share * rep_count == out_weight.shape[1]:
+        own_share = lax.dynamic_slice_in_dim(
+            out_weight, lax.axis_index("rep") * share, share, 1
+        )
+        full_weight = lax.all_gather(own_share, ("ctx", "rep"), axis=1, tiled=True)
+    else:
+        full_weight = lax.all_gather(out_weight, "ctx", axis=1, tiled=True)
     local_seqs = queries.shape[0]
     tokens = queries.shape[1]
     row_count = local_seqs * tokens
@@ -238,24 +243,10 @@
         .reshape(row_count, q_local * head_dim)
         .astype(jnp.bfloat16)
     )
-    partial_proj = jnp.dot(
-        attended,
-        lax.all_gather(out_weight, "ctx", axis=1, tiled=True),
-        preferred_element_type=jnp.float32,
-    )
-    own_stream = stream.reshape(row_count, col_width).astype(jnp.float32)
-    summed = lax.psum_scatter(
-        partial_proj.astype(jnp.bfloat16), "head", scatter_dimension=1, tiled=True
-    )
-    own_state = (summed.astype(jnp.float32) + own_stream).astype(jnp.bfloat16)
-    width = norm_gain.shape[0]
-    every_state = lax.all_gather(own_state, ("ctx", "head"), axis=0, tiled=False)
-    every_state = every_state.reshape(ctx_count, width // col_width, row_count, col_width)
-    all_rows = ctx_count * row_count
-    expert_count = router.shape[1]
     token_ids = lax.all_gather(
         expert_ids.reshape(row_count, expert_ids.shape[2]).T, "ctx", axis=1, tiled=True
     )
+    all_rows = ctx_count * row_count
     halves = w_gate_up.shape[0]
     units = w_gate_up.shape[1]
     token_block = min(all_rows, 8 * tokens)
@@ -265,6 +256,17 @@
     counted = named.astype(jnp.int32).reshape(halves, all_rows // token_block, token_block)
     rank = jnp.cumsum(counted, axis=2) - 1
     slots = jnp.where(named, rank.reshape(halves, all_rows), -1).reshape(halves, 1, all_rows)
+    attended, slots, token_ids = lax.optimization_barrier((attended, slots, token_ids))
+    partial_proj = jnp.dot(attended, full_weight, preferred_element_type=jnp.float32)
+    own_stream = stream.reshape(row_count, col_width).astype(jnp.float32)
+    summed = lax.psum_scatter(
+        partial_proj.astype(jnp.bfloat16), "head", scatter_dimension=1, tiled=True
+    )
+    own_state = (summed.astype(jnp.float32) + own_stream).astype(jnp.bfloat16)
+    width = norm_gain.shape[0]
+    every_state = lax.all_gather(own_state, ("ctx", "head"), axis=0, tiled=False)
+    every_state = every_state.reshape(ctx_count, width // col_width, row_count, col_width)
+    expert_count = router.shape[1]
     unit_rows = jnp.transpose(w_gate_up, (1, 0, 2)).reshape(units * halves, w_gate_up.shape[2])
     router_rows = jnp.pad(router.T, ((0, 0), (0, -width % LANES)))
     gain = norm_gain.reshape(width // col_width, 1, col_width)
@@ -277,7 +279,8 @@
     chosen_rows = (row_expert[:, None] == jnp.arange(expert_count)[None, :]).astype(jnp.float32)
     mix_rows = jnp.dot(chosen_rows, mix_all, precision=lax.Precision.HIGHEST)
     mix_rows = mix_rows.reshape(halves, 1, all_rows)
-    every_active = lax.all_gather(active, "head", axis=0, tiled=False)
+    every_active = lax.all_gather(active.reshape(-1, units), "head", axis=0, tiled=True)
+    every_active = every_active.reshape(width // col_width, *active.shape)
     partial_out = down_call(every_active, w_down, slots, mix_rows, token_block)
     combined = lax.psum_scatter(partial_out, "ctx", scatter_dimension=0, tiled=True)
     layer_out = (own_state.astype(jnp.float32) + combined.astype(jnp.float32)).astype(jnp.bfloat16)

time: 262 us -> 248 us (0.947)
  Pallas kernels: 48.4 us -> 42.4 us
  local copies, waits for them, and re-layouts: 15.1 us -> 10.5 us
  waiting for transfers between devices: 145 us -> 141 us
    all_gather x2, waiting for transfers between devices: 68.6 us -> 51.1 us  [the longest x1 27 us: on_device(): full_weight = lax.all_gather(own_share, ('ctx', 'rep'), axis=1, tiled=True)]
    all_gather x1, waiting for transfers between devices: 30.1 us -> 44.5 us  [on_device(): lax.all_gather(own_state, ('ctx', 'head'), axis=0, tiled=False)]
    pallas_call x1, Pallas kernels: 19.9 us -> 13.1 us  [down_call(): pl.pallas_call(down_kernel, grid=(blocks, halves // pair), out_shape=jax....]
    all_gather x1 -> x0, local copies, waits for them, and re-layouts: 4.22 us -> none  [on_device(): every_active = lax.all_gather(active, 'head', axis=0, tiled=False)]
    pallas_call x1 -> x0, local copies, waits for them, and re-layouts: 2.69 us -> none  [gate_up_call(): pl.pallas_call(functools.partial(gate_up_kernel, halves, units), grid=(bl...]
    unnamed x21 -> x19, local copies, waits for them, and re-layouts: 4.01 us -> 5.58 us
  transfers between devices with their start and end apart: 5 -> 5, of which waited for: 5 -> 5; matrix products, arithmetic and copies ran while one was open for 4% -> 5% of each run, Pallas kernels for 0% -> 0%
where the time goes in v2:
time: 248 us
  waiting for transfers between devices  141 us (57%)
  Pallas kernels  42.4 us (17%)
  blocking collectives  27.8 us (11%)
  between operations  13.3 us (5%)
  local copies, waits for them, and re-layouts  10.5 us (4%)
  other arithmetic  7.36 us (3%)
  matrix products  5.34 us (2%)
    all_gather x1, waiting for transfers between devices, on_device(): lax.all_gather(own_state, ('ctx', 'head'), axis=0, tiled=False)  44.5 us
    pallas_call x1, Pallas kernels, gate_up_call(): pl.pallas_call(functools.partial(gate_up_kernel, halves, units), grid=(bl...  29.3 us
    all_gather x1, waiting for transfers between devices, on_device(): full_weight = lax.all_gather(own_share, ('ctx', 'rep'), axis=1, tiled=True)  27 us
    all_gather x1, waiting for transfers between devices, on_device(): lax.all_gather(active.reshape(-1, units), 'head', axis=0, tiled=True)  24.1 us
    reduce_scatter x1, waiting for transfers between devices, on_device(): lax.psum_scatter(partial_out, 'ctx', scatter_dimension=0, tiled=True)  23.3 us
    unnamed x6, waiting for transfers between devices  21.7 us
    all_gather x1, blocking collectives, on_device(): shard_piece = lax.all_gather(keyvals, 'ctx', axis=1, tiled=True)  14.2 us
    all_gather x1, blocking collectives, on_device(): lax.all_gather(expert_ids.reshape(row_count, expert_ids.shape[2]).T, 'ctx...  13.6 us
  transfers between devices with their start and end apart: 5, of which 5 were waited for; matrix products, arithmetic and copies ran while one was open for 5% of the time, Pallas kernels for 0%

profile of v2, /device:TPU:0, one launch (start us, length us, event | category | flops | bytes accessed | tf_op | source)
XLA Modules:
  0.0 247.6 jit_solution(6345930171015570247)
XLA Ops:
  6.5 1.1 copy-done
  7.7 0.8 constant_dynamic-slice_fusion
  8.4 0.0 reduce-scatter.7.cloned.1.call-start
  8.5 0.7 copy.42
  9.2 0.1 reshape.289
  9.3 13.6 %all_gather.19 = s32[4,512]{1,0:T(4,128)S(1)} all-gather(s32[4,128]{1,0:T(4,128)S(1)} %bitcast.75), channel_id=1, replica_groups=mesh['ctx'=4,'head'=4,'rep'=2] {'ctx'}, dimensions={1}, use_global_device_ids=true | all-gather | bytes 10240 | tf_op jit(solution)/shard_map/all_gather | solution.py:246
  22.9 0.1 compare_reduce_fusion
  23.1 1.2 reduce-window.6
  24.2 0.2 slice_reduce_fusion
  24.5 0.1 copy.45
  24.6 0.9 broadcast_multiply_fusion
  25.5 0.2 reshape.288
  25.7 0.8 copy.38
  26.5 14.2 %all_gather.18 = bf16[2,256,1,128]{3,0,2,1:T(2,128)(2,1)S(1)} all-gather(bf16[2,64,1,128]{3,0,2,1:T(2,128)(2,1)S(1)} %copy.38), channel_id=1, replica_groups=mesh['ctx'=4,'head'=4,'rep'=2] {'ctx'}, dimensions={1}, use_global_device_ids=true | all-gather | bytes 163840 | tf_op jit(solution)/shard_map/all_gather | solution.py:227
  40.7 2.4 conditional.1
  40.7 0.1 copy.39
  40.8 0.2 copy.40
  41.0 0.2 reshape.273
  41.3 0.1 add.70
  41.3 0.1 iota_compare_fusion
  41.4 0.4 fusion.18
  41.8 0.7 broadcast_in_dim.29
  42.5 0.1 broadcast_in_dim.30
  42.6 0.3 fusion
  42.9 0.2 fusion.2
  43.1 0.2 convert_element_type.61
  43.4 0.2 copy.41
  43.6 0.2 convert_element_type.63
  43.8 0.1 broadcast.171
  43.9 0.7 copy_select_fusion.slot_ref
  44.6 27.0 %all-gather.5.cloned.1.call-done = bf16[512,2880]{0,1:T(8,128)(2,1)} async-done(((bf16[512,360]{0,1:T(8,128)(2,1)}), bf16[512,2880]{0,1:T(8,128)(2,1)}) %all-gather.5.cloned.1.call-update) | async-done | bytes 2949136 | tf_op jit(solution)/shard_map/all_gather | solution.py:176
  71.5 3.6 %fusion.7 = bf16[2880,128]{1,0:T(8,128)(2,1)} fusion(bf16[128,512]{1,0:T(8,128)(2,1)S(1)} %convert_element_type.63, bf16[512,2880]{0,1:T(8,128)(2,1)} %all-gather.5.cloned.1.call-done), kind=kOutput, calls=%fused_computation.18 | convolution fusion | flops 377856000 | bytes 3817472 | tf_op jit(solution)/shard_map/dot_general | solution.py:260
  75.2 0.0 all-gather.9.cloned.1.call-start
  75.3 21.7 %reduce-scatter.7.cloned.1.call-done = bf16[720,128]{1,0:T(8,128)(2,1)} async-done(((bf16[2880,128]{1,0:T(8,128)(2,1)}), bf16[720,128]{1,0:T(8,128)(2,1)}) %reduce-scatter.7.cloned.1.call-update) | async-done | bytes 184336
  96.9 1.1 copy.49
  98.0 0.7 fusion.8
  98.8 0.7 reshape.295.gain_ref
  99.5 0.7 pad.4.router_ref
  100.2 44.5 %all-gather.9.cloned.1.call-done = bf16[2048,720]{1,0:T(8,128)(2,1)} async-done(((bf16[128,720]{1,0:T(8,128)(2,1)}), bf16[2048,720]{1,0:T(8,128)(2,1)}) %all-gather.9.cloned.1.call-update) | async-done | bytes 2949136 | tf_op jit(solution)/shard_map/all_gather | solution.py:267
  144.7 29.3 %shard_map.101 = (bf16[16,1,96,180]{3,2,1,0:T(8,128)(2,1)}, f32[32,512]{1,0:T(8,128)}) custom-call(bf16[4,4,128,720]{3,2,1,0:T(8,128)(2,1)} %bitcast.65, f32[4,1,720]{2,1,0:T(1,128)} %reshape.295.gain_ref, bf16[32,2944]{1,0:T(8,128)(2,1)} %pad.4.router_ref, bf16[2880,5760]{1,0:T(8,128)(2,1)} %bitcast.64, s32[16,1,512]{2,1,0:T(1,128)} %copy_select_fusion.slot_ref), custom_call_target="tpu_custom_call" | custom-call | tf_op jit(solution)/shard_map/pallas_call | solution.py:93
  174.2 0.9 fusion.15
  175.0 0.9 fusion.12
  175.9 1.0 fusion.10
  177.0 24.1 %all-gather.7.cloned.1.call-done = bf16[6144,180]{1,0:T(8,128)(2,1)} async-done(((bf16[1536,180]{1,0:T(8,128)(2,1)}), bf16[6144,180]{1,0:T(8,128)(2,1)}) %all-gather.7.cloned.1.call-update) | async-done | bytes 2211856 | tf_op jit(solution)/shard_map/all_gather | solution.py:282
  201.1 1.9 copy-done.2
  203.0 13.1 %shard_map.102 = bf16[512,720]{1,0:T(8,128)(2,1)} custom-call(bf16[4,16,1,96,180]{4,3,2,1,0:T(8,128)(2,1)S(1)} %bitcast.63, bf16[16,720,720]{2,1,0:T(8,128)(2,1)} %w_ref.1, s32[16,1,512]{2,1,0:T(1,128)S(1)} %copy-done.3, f32[16,1,512]{2,1,0:T(1,128)S(1)} %reshape.299.mix_ref), custom_call_target="tpu_custom_call" | custom-call | tf_op jit(solution)/shard_map/pallas_call | solution.py:150
  216.1 23.3 %reduce-scatter.5.cloned.1.call-done = bf16[128,720]{1,0:T(8,128)(2,1)} async-done(((bf16[512,720]{1,0:T(8,128)(2,1)}), bf16[128,720]{1,0:T(8,128)(2,1)}) %reduce-scatter.5.cloned.1.call-update) | async-done | bytes 184336 | tf_op jit(solution)/shard_map/reduce_scatter | solution.py:285
  239.4 1.6 add_convert_fusion
  (36 shorter events, 0.4 us)
Async XLA Ops:
  6.5 1.1 copy-start
  6.5 65.0 %all-gather.5.cloned.1.call-start = ((), (), s32[]{:S(2)}) async-start(), calls=%async_computation.2 | async-start | bytes 3317760 | tf_op jit(solution)/shard_map/all_gather | solution.py:176
  8.4 88.5 %reduce-scatter.7.cloned.1.call-start = ((), (), s32[]{:S(2)}) async-start(), calls=%async_computation.6 | async-start | bytes 921600
  43.3 54.6 %copy-start.5 = (bf16[2,64,720]{2,1,0:T(8,128)(2,1)S(1)}, bf16[2,64,720]{2,1,0:T(8,128)(2,1)}, u32[]{:S(2)}) copy-start(bf16[2,64,720]{2,1,0:T(8,128)(2,1)} %param.15) | copy-start | bytes 552964
  43.8 55.0 %copy-start.7 = (f32[2880]{0:T(1024)S(1)}, f32[2880]{0:T(1024)}, u32[]{:S(2)}) copy-start(f32[2880]{0:T(1024)} %param.17) | copy-start | bytes 34564
  43.8 55.7 %copy-start.6 = (bf16[2880,32]{0,1:T(8,128)(2,1)S(1)}, bf16[2880,32]{0,1:T(8,128)(2,1)}, u32[]{:S(2)}) copy-start(bf16[2880,32]{0,1:T(8,128)(2,1)} %param.18) | copy-start | bytes 552964
  75.2 69.5 %all-gather.9.cloned.1.call-start = ((), (), s32[]{:S(2)}) async-start(), calls=%async_computation.5 | async-start | bytes 3342336 | tf_op jit(solution)/shard_map/all_gather | solution.py:267
  98.7 102.3 %all-gather.7.cloned.1.call-start = ((), (), s32[]{:S(2)}) async-start(), calls=%async_computation.3 | async-start | bytes 3932160 | tf_op jit(solution)/shard_map/all_gather | solution.py:282
  144.7 56.4 %copy-start.3 = (s32[16,1,512]{2,1,0:T(1,128)S(1)}, s32[16,1,512]{2,1,0:T(1,128)}, u32[]{:S(2)}) copy-start(s32[16,1,512]{2,1,0:T(1,128)} %copy_select_fusion.slot_ref) | copy-start | bytes 98308
  174.1 65.3 %reduce-scatter.5.cloned.1.call-start = ((), (), s32[]{:S(2)}) async-start(), calls=%async_computation.4 | async-start | bytes 983040 | tf_op jit(solution)/shard_map/reduce_scatter | solution.py:285
  201.1 1.9 copy-start.2
  203.0 36.4 %copy-start.4 = (bf16[128,720]{1,0:T(8,128)(2,1)S(1)}, bf16[128,720]{1,0:T(8,128)(2,1)}, u32[]{:S(2)}) copy-start(bf16[128,720]{1,0:T(8,128)(2,1)} %fusion.8) | copy-start | bytes 552964
  203.0 38.0 %copy-start.1 = (bf16[512,720]{0,1:T(8,128)(2,1)S(1)}, bf16[512,720]{0,1:T(8,128)(2,1)}, u32[]{:S(2)}) copy-start(bf16[512,720]{0,1:T(8,128)(2,1)} %param.16) | copy-start | bytes 2211844
Sparse Core Ops, SparseCore 0:
  9.5 61.9 all-gather.4
  75.3 21.5 reduce-scatter.6
  99.2 45.4 all-gather.8
  174.2 26.8 all-gather.6
  216.2 23.1 reduce-scatter.4

commit v3 on v2

--- a/solution.py
+++ b/solution.py
@@ -167,15 +167,6 @@
     queries, keyvals, sinks, stream, out_weight, norm_gain, router, expert_ids, w_gate_up, w_down
 ):
     ctx_count = lax.axis_size("ctx")
-    rep_count = lax.axis_size("rep")
-    share = out_weight.shape[1] // rep_count
-    if share * rep_count == out_weight.shape[1]:
-        own_share = lax.dynamic_slice_in_dim(
-            out_weight, lax.axis_index("rep") * share, share, 1
-        )
-        full_weight = lax.all_gather(own_share, ("ctx", "rep"), axis=1, tiled=True)
-    else:
-        full_weight = lax.all_gather(out_weight, "ctx", axis=1, tiled=True)
     local_seqs = queries.shape[0]
     tokens = queries.shape[1]
     row_count = local_seqs * tokens
@@ -256,15 +247,35 @@
     counted = named.astype(jnp.int32).reshape(halves, all_rows // token_block, token_block)
     rank = jnp.cumsum(counted, axis=2) - 1
     slots = jnp.where(named, rank.reshape(halves, all_rows), -1).reshape(halves, 1, all_rows)
-    attended, slots, token_ids = lax.optimization_barrier((attended, slots, token_ids))
-    partial_proj = jnp.dot(attended, full_weight, preferred_element_type=jnp.float32)
-    own_stream = stream.reshape(row_count, col_width).astype(jnp.float32)
-    summed = lax.psum_scatter(
-        partial_proj.astype(jnp.bfloat16), "head", scatter_dimension=1, tiled=True
-    )
-    own_state = (summed.astype(jnp.float32) + own_stream).astype(jnp.bfloat16)
     width = norm_gain.shape[0]
-    every_state = lax.all_gather(own_state, ("ctx", "head"), axis=0, tiled=False)
+    head_count = lax.axis_size("head")
+    swapped = ctx_count == head_count and out_weight.shape[1] == col_width
+    if swapped:
+        pairs = [
+            (first * head_count + second, second * head_count + first)
+            for first in range(ctx_count)
+            for second in range(head_count)
+        ]
+        turned = lax.ppermute(
+            stream.reshape(row_count, col_width), ("ctx", "head"), perm=pairs
+        )
+        every_row = lax.all_gather(attended, "ctx", axis=0, tiled=True)
+        partial_proj = jnp.dot(every_row, out_weight, preferred_element_type=jnp.float32)
+        summed = lax.psum_scatter(
+            partial_proj.astype(jnp.bfloat16), "head", scatter_dimension=0, tiled=True
+        )
+        turned_state = summed.astype(jnp.float32) + turned.astype(jnp.float32)
+        every_state = lax.all_gather(
+            turned_state.astype(jnp.bfloat16), ("head", "ctx"), axis=0, tiled=False
+        )
+    else:
+        partial_proj = jnp.dot(attended, lax.all_gather(out_weight, "ctx", axis=1, tiled=True), preferred_element_type=jnp.float32)
+        own_stream = stream.reshape(row_count, col_width).astype(jnp.float32)
+        summed = lax.psum_scatter(
+            partial_proj.astype(jnp.bfloat16), "head", scatter_dimension=1, tiled=True
+        )
+        own_state = (summed.astype(jnp.float32) + own_stream).astype(jnp.bfloat16)
+        every_state = lax.all_gather(own_state, ("ctx", "head"), axis=0, tiled=False)
     every_state = every_state.reshape(ctx_count, width // col_width, row_count, col_width)
     expert_count = router.shape[1]
     unit_rows = jnp.transpose(w_gate_up, (1, 0, 2)).reshape(units * halves, w_gate_up.shape[2])
@@ -283,6 +294,8 @@
     every_active = every_active.reshape(width // col_width, *active.shape)
     partial_out = down_call(every_active, w_down, slots, mix_rows, token_block)
     combined = lax.psum_scatter(partial_out, "ctx", scatter_dimension=0, tiled=True)
+    if swapped:
+        own_state = every_state[lax.axis_index("ctx"), lax.axis_index("head")]
     layer_out = (own_state.astype(jnp.float32) + combined.astype(jnp.float32)).astype(jnp.bfloat16)
     return layer_out.reshape(local_seqs, tokens, col_width)
 

time: 248 us -> 220 us (0.89)
  waiting for transfers between devices: 141 us -> 101 us
  blocking collectives: 27.8 us -> 43.2 us
  matrix products: 5.34 us -> 2.28 us
    all_gather x2 -> x1, waiting for transfers between devices: 71.5 us -> 30.2 us  [on_device(): lax.all_gather(turned_state.astype(jnp.bfloat16), ('head', 'ctx'), axis=0...]
    reduce_scatter x0 -> x1, waiting for transfers between devices: none -> 23 us  [on_device(): lax.psum_scatter(partial_proj.astype(jnp.bfloat16), 'head', scatter_dimen...]
    unnamed x6 -> x4, waiting for transfers between devices: 21.7 us -> 0.07 us
    all_gather x0 -> x1, blocking collectives: none -> 16.1 us  [on_device(): every_row = lax.all_gather(attended, 'ctx', axis=0, tiled=True)]
    dot_general x1, matrix products: 3.63 us -> 0.57 us  [on_device(): jnp.dot(every_row, out_weight, preferred_element_type=jnp.float32)]
    unnamed x19 -> x17, local copies, waits for them, and re-layouts: 5.58 us -> 3.87 us
  transfers between devices with their start and end apart: 5 -> 5, of which waited for: 5 -> 4; matrix products, arithmetic and copies ran while one was open for 5% -> 3% of each run, Pallas kernels for 0% -> 0%
where the time goes in v3:
time: 220 us; the launch traced here: 219 us
  waiting for transfers between devices  101 us (46%)
  blocking collectives  43.2 us (20%)
  Pallas kernels  42.3 us (19%)
  between operations  13.3 us (6%)
  other arithmetic  8.43 us (4%)
  local copies, waits for them, and re-layouts  8.04 us (4%)
  matrix products  2.28 us (1%)
    all_gather x1, waiting for transfers between devices, on_device(): lax.all_gather(turned_state.astype(jnp.bfloat16), ('head', 'ctx'), axis=0...  30.2 us
    pallas_call x1, Pallas kernels, gate_up_call(): pl.pallas_call(functools.partial(gate_up_kernel, halves, units), grid=(bl...  29.3 us
    all_gather x1, waiting for transfers between devices, on_device(): lax.all_gather(active.reshape(-1, units), 'head', axis=0, tiled=True)  24.1 us
    reduce_scatter x1, waiting for transfers between devices, on_device(): lax.psum_scatter(partial_out, 'ctx', scatter_dimension=0, tiled=True)  23.3 us
    reduce_scatter x1, waiting for transfers between devices, on_device(): lax.psum_scatter(partial_proj.astype(jnp.bfloat16), 'head', scatter_dimen...  23 us
    all_gather x1, blocking collectives, on_device(): every_row = lax.all_gather(attended, 'ctx', axis=0, tiled=True)  16.1 us
    all_gather x1, blocking collectives, on_device(): shard_piece = lax.all_gather(keyvals, 'ctx', axis=1, tiled=True)  15.1 us
    pallas_call x1, Pallas kernels, down_call(): pl.pallas_call(down_kernel, grid=(blocks, halves // pair), out_shape=jax....  13 us
  transfers between devices with their start and end apart: 5, of which 4 were waited for; matrix products, arithmetic and copies ran while one was open for 3% of the time, Pallas kernels for 0%

profile of v3, /device:TPU:0, one launch (start us, length us, event | category | flops | bytes accessed | tf_op | source)
XLA Modules:
  0.0 219.1 jit_solution(6090324159182915267)
XLA Ops:
  6.5 1.0 broadcast_multiply_fusion
  7.5 0.2 reshape.289
  7.7 0.8 copy.40
  8.5 15.1 %all_gather.18 = bf16[2,256,1,128]{3,0,2,1:T(2,128)(2,1)S(1)} all-gather(bf16[2,64,1,128]{3,0,2,1:T(2,128)(2,1)S(1)} %copy.40), channel_id=1, replica_groups=mesh['ctx'=4,'head'=4,'rep'=2] {'ctx'}, dimensions={1}, use_global_device_ids=true | all-gather | bytes 163840 | tf_op jit(solution)/shard_map/all_gather | solution.py:218
  23.6 2.4 %conditional.1 = (f32[2,1,512]{2,0,1:T(2,128)S(1)}, f32[2,1,64,512]{3,2,0,1:T(8,128)S(1)}) conditional(s32[]{:T(128)} %convert_element_type.59, (f32[8]{0:T(128)}, s32[]{:T(128)}, s32[8,64]{1,0:T(8,128)S(1)}, bf16[2,256,1,128]{3,0,2,1:T(2,128)(2,1)S(1)}, bf16[2,1,8,64,64]{4,2,3,0,1:T(8,128)(2,1)S(1)}) %tuple.30, () %tuple.14), branch_computations={%region_0.3_spmd, %region_3.4_spmd} | conditional | flops 68882944 | bytes 4784180 | solution.py:226
  23.6 0.1 copy.41
  23.7 0.2 copy.42
  24.0 0.2 reshape.273
  24.2 0.1 add.72
  24.3 0.1 iota_compare_fusion
  24.4 0.4 fusion.17
  24.7 0.7 broadcast_in_dim.29
  25.5 0.1 broadcast_in_dim.30
  25.6 0.3 fusion
  25.9 0.2 fusion.2
  26.1 0.2 convert_element_type.61
  26.3 0.2 copy.43
  26.6 0.2 convert_element_type.63
  26.8 16.1 %all_gather.19 = bf16[512,512]{1,0:T(8,128)(2,1)S(1)} all-gather(bf16[128,512]{1,0:T(8,128)(2,1)S(1)} %convert_element_type.63), channel_id=1, replica_groups=mesh['ctx'=4,'head'=4,'rep'=2] {'ctx'}, dimensions={0}, use_global_device_ids=true | all-gather | bytes 655360 | tf_op jit(solution)/shard_map/all_gather | solution.py:262
  42.9 0.6 convolution_convert_fusion
  43.5 1.2 copy.50
  44.7 0.0 all-gather.6.cloned.1.call-start
  44.7 0.7 collective-permute-start
  45.4 23.0 %reduce-scatter.7.cloned.1.call-done = bf16[128,720]{1,0:T(8,128)(2,1)} async-done(((bf16[512,720]{1,0:T(8,128)(2,1)}), bf16[128,720]{1,0:T(8,128)(2,1)}) %reduce-scatter.7.cloned.1.call-update) | async-done | bytes 184336 | tf_op jit(solution)/shard_map/reduce_scatter | solution.py:264
  68.4 1.6 add_convert_fusion
  70.1 0.0 all-gather.4.cloned.1.call-start
  70.2 0.1 reshape.294
  70.3 12.0 %all_gather.22 = s32[4,512]{1,0:T(4,128)S(1)} all-gather(s32[4,128]{1,0:T(4,128)S(1)} %bitcast.74), channel_id=1, replica_groups=mesh['ctx'=4,'head'=4,'rep'=2] {'ctx'}, dimensions={1}, use_global_device_ids=true | all-gather | bytes 10240 | tf_op jit(solution)/shard_map/all_gather | solution.py:237
  82.2 0.1 compare_reduce_fusion
  82.4 1.2 reduce-window.6
  83.6 0.2 slice_reduce_fusion
  83.8 0.1 copy.48
  83.9 0.7 reshape.292.gain_ref
  84.6 0.7 pad.4.router_ref
  85.3 0.1 broadcast.170
  85.4 0.7 copy_select_fusion.slot_ref
  86.0 30.2 %all-gather.6.cloned.1.call-done = bf16[2048,720]{1,0:T(8,128)(2,1)} async-done(((bf16[128,720]{1,0:T(8,128)(2,1)}), bf16[2048,720]{1,0:T(8,128)(2,1)}) %all-gather.6.cloned.1.call-update) | async-done | bytes 2949136 | tf_op jit(solution)/shard_map/all_gather | solution.py:268
  116.2 29.3 %shard_map.101 = (bf16[16,1,96,180]{3,2,1,0:T(8,128)(2,1)}, f32[32,512]{1,0:T(8,128)}) custom-call(bf16[4,4,128,720]{3,2,1,0:T(8,128)(2,1)} %bitcast.64, f32[4,1,720]{2,1,0:T(1,128)} %reshape.292.gain_ref, bf16[32,2944]{1,0:T(8,128)(2,1)} %pad.4.router_ref, bf16[2880,5760]{1,0:T(8,128)(2,1)} %bitcast.63, s32[16,1,512]{2,1,0:T(1,128)} %copy_select_fusion.slot_ref), custom_call_target="tpu_custom_call" | custom-call | tf_op jit(solution)/shard_map/pallas_call | solution.py:93
  145.5 0.0 all-gather.4.cloned.1.call-update
  145.5 0.0 reduce-scatter.5.cloned.1.call-start
  145.6 0.9 fusion.14
  146.5 0.9 fusion.11
  147.4 1.0 fusion.9
  148.4 24.1 %all-gather.4.cloned.1.call-done = bf16[6144,180]{1,0:T(8,128)(2,1)} async-done(((bf16[1536,180]{1,0:T(8,128)(2,1)}), bf16[6144,180]{1,0:T(8,128)(2,1)}) %all-gather.4.cloned.1.call-update) | async-done | bytes 2211856 | tf_op jit(solution)/shard_map/all_gather | solution.py:293
  172.5 1.9 copy-done.1
  174.4 13.0 %shard_map.102 = bf16[512,720]{1,0:T(8,128)(2,1)} custom-call(bf16[4,16,1,96,180]{4,3,2,1,0:T(8,128)(2,1)S(1)} %bitcast.62, bf16[16,720,720]{2,1,0:T(8,128)(2,1)} %w_ref.1, s32[16,1,512]{2,1,0:T(1,128)S(1)} %copy-done.2, f32[16,1,512]{2,1,0:T(1,128)S(1)} %reshape.301.mix_ref), custom_call_target="tpu_custom_call" | custom-call | tf_op jit(solution)/shard_map/pallas_call | solution.py:150
  187.4 23.3 %reduce-scatter.5.cloned.1.call-done = bf16[128,720]{1,0:T(8,128)(2,1)} async-done(((bf16[512,720]{1,0:T(8,128)(2,1)}), bf16[128,720]{1,0:T(8,128)(2,1)}) %reduce-scatter.5.cloned.1.call-update) | async-done | bytes 184336 | tf_op jit(solution)/shard_map/reduce_scatter | solution.py:296
  210.8 1.7 fusion.7
  (33 shorter events, 0.3 us)
Async XLA Ops:
  6.5 36.4 %copy-start = (bf16[512,720]{0,1:T(8,128)(2,1)S(1)}, bf16[512,720]{0,1:T(8,128)(2,1)}, u32[]{:S(2)}) copy-start(bf16[512,720]{0,1:T(8,128)(2,1)} %param.16) | copy-start | bytes 2211844
  6.5 61.9 %reduce-scatter.7.cloned.1.call-start = ((), (), s32[]{:S(2)}) async-start(), calls=%async_computation.5 | async-start | bytes 983040 | tf_op jit(solution)/shard_map/reduce_scatter | solution.py:264
  26.1 18.6 %copy-start.6 = (bf16[2,64,720]{2,1,0:T(8,128)(2,1)S(1)}, bf16[2,64,720]{2,1,0:T(8,128)(2,1)}, u32[]{:S(2)}) copy-start(bf16[2,64,720]{2,1,0:T(8,128)(2,1)} %param.15) | copy-start | bytes 552964
  26.5 43.6 %copy-start.5 = (s32[2,64,4]{1,2,0:T(4,128)S(1)}, s32[2,64,4]{1,2,0:T(4,128)}, u32[]{:S(2)}) copy-start(s32[2,64,4]{1,2,0:T(4,128)} %param.19) | copy-start | bytes 6148
  26.8 57.1 %copy-start.4 = (f32[2880]{0:T(1024)S(1)}, f32[2880]{0:T(1024)}, u32[]{:S(2)}) copy-start(f32[2880]{0:T(1024)} %param.17) | copy-start | bytes 34564
  26.8 57.8 %copy-start.3 = (bf16[2880,32]{0,1:T(8,128)(2,1)S(1)}, bf16[2880,32]{0,1:T(8,128)(2,1)}, u32[]{:S(2)}) copy-start(bf16[2880,32]{0,1:T(8,128)(2,1)} %param.18) | copy-start | bytes 552964
  44.7 71.5 %all-gather.6.cloned.1.call-start = ((), (), s32[]{:S(2)}) async-start(), calls=%async_computation.4 | async-start | bytes 3342336 | tf_op jit(solution)/shard_map/all_gather | solution.py:268
  44.7 0.7 collective-permute-start
  70.1 102.4 %all-gather.4.cloned.1.call-start = ((), (), s32[]{:S(2)}) async-start(), calls=%async_computation.2 | async-start | bytes 3932160 | tf_op jit(solution)/shard_map/all_gather | solution.py:293
  116.2 56.4 %copy-start.2 = (s32[16,1,512]{2,1,0:T(1,128)S(1)}, s32[16,1,512]{2,1,0:T(1,128)}, u32[]{:S(2)}) copy-start(s32[16,1,512]{2,1,0:T(1,128)} %copy_select_fusion.slot_ref) | copy-start | bytes 98308
  145.5 65.2 %reduce-scatter.5.cloned.1.call-start = ((), (), s32[]{:S(2)}) async-start(), calls=%async_computation.3 | async-start | bytes 983040 | tf_op jit(solution)/shard_map/reduce_scatter | solution.py:296
  172.5 1.9 copy-start.1
Sparse Core Ops, SparseCore 0:
  44.8 23.6 reduce-scatter.6
  70.8 45.3 all-gather.5
  145.7 26.8 all-gather.3
  187.6 23.1 reduce-scatter.4
